TPU v7x, 32 devices: a whole 2x2x4 slice. The times are simulated.
32 devices in a mesh: groups: 2 (over y), view: 4 (over z), row: 4 (over x, core).
Axes of the slice: x: 2, y: 2, z: 4, core: 2. Of those that a mesh axis runs over, the one named last changes fastest.
Arguments:
- inputs: bfloat16 [64, 292, 16, 16], P(None, 'view', ('groups', 'row')), parts along dimension 2, may hold values from -24 to 24
- cotangent: bfloat16 [64, 292, 16, 16], P(None, None, ('groups', 'row'), 'view'), parts along dimension 2, may hold values from -6 to 6
- keep: int32 [584], P('groups'), parts along dimension 0, may hold values from 0 to 1, as said below
- w_conv: bfloat16 [64, 64, 3, 3], replicated, may hold values from -0.25 to 0.25
- gain: float32 [64], replicated, may hold values from 0.5 to 1.5
- w_query: bfloat16 [64, 64], replicated, may hold values from -3 to 3
- w_key: bfloat16 [64, 64], replicated, may hold values from -3 to 3
- w_value: bfloat16 [64, 64], replicated, may hold values from -0.75 to 0.75
- w_out: bfloat16 [64, 64], replicated, may hold values from -0.75 to 0.75
Outputs:
- output: bfloat16 [64, 292, 16, 16], P(None, None, ('groups', 'row'), 'view'), parts along dimension 2
- d_input: bfloat16 [64, 292, 16, 16], P(None, 'view', ('groups', 'row')), parts along dimension 2
- g_conv: float32 [128, 64, 3, 3], P('groups'), parts along dimension 0
- g_gain: float32 [128], P('groups'), parts along dimension 0
- g_query: float32 [128, 64], P('groups'), parts along dimension 0
- g_key: float32 [128, 64], P('groups'), parts along dimension 0
- g_value: float32 [128, 64], P('groups'), parts along dimension 0
- g_out: float32 [128, 64], P('groups'), parts along dimension 0
There are 2 independent parts, one for each index of `groups`. A program takes and returns all parts, laid end to end along the dimension named above; an argument that names none is the same for every part. Nothing has to cross between parts.
Inputs may be any that keep to these rules, and one draw needn't show every extreme that they name: `keep`: zero at every view from 289 on, one at view 289 // 2.
All inputs are finite; a program needn't handle non-finite values.
Results may differ from a plain program's by a relative error of at most 0.012.
The roundings to bfloat16 on the way count: a program that leaves them out, or rounds other values in their place, can miss the bound.
Values may be sent and summed in bfloat16 or wider, within the bound.
No kernel may reach another device: no remote copies, remote signals or barrier semaphores. Data moves between devices by JAX's collectives and lax.ppermute only.
A program may use at most 64 MiB of HBM per device.

v0:
```python
import math
import jax
import jax.numpy as jnp
from jax import lax
from jax.sharding import PartitionSpec as P


def with_halo(cells, sides, width):
    for axis, dim in sides:
        count = lax.axis_size(axis)
        ends = count - 1
        head = lax.slice_in_dim(cells, 0, width, axis=dim)
        tail = lax.slice_in_dim(cells, cells.shape[dim] - width, cells.shape[dim], axis=dim)
        cells = jnp.concatenate(
            [
                lax.ppermute(tail, axis, [(i, (i + 1) % count) for i in range(ends)]),
                cells,
                lax.ppermute(head, axis, [((i + 1) % count, i) for i in range(ends)]),
            ],
            axis=dim,
        )
    return cells


def product(form, left, right):
    return jnp.einsum(form, left, right, preferred_element_type=jnp.float32)


def convolve(padded, w_conv):
    height = padded.shape[2] - 2
    breadth = padded.shape[3] - 2
    total = jnp.zeros((w_conv.shape[0], padded.shape[1], height, breadth), jnp.float32)
    for row_tap in range(3):
        for col_tap in range(3):
            window = padded[:, :, row_tap : row_tap + height, col_tap : col_tap + breadth]
            total = total + product("oc,cvrw->ovrw", w_conv[:, :, row_tap, col_tap], window)
    return total


def input_grad(grad_pad, w_conv):
    height = grad_pad.shape[2] - 2
    breadth = grad_pad.shape[3] - 2
    total = jnp.zeros((w_conv.shape[1], grad_pad.shape[1], height, breadth), jnp.float32)
    for row_tap in range(3):
        for col_tap in range(3):
            window = grad_pad[
                :, :, 2 - row_tap : 2 - row_tap + height, 2 - col_tap : 2 - col_tap + breadth
            ]
            total = total + product("oc,ovrw->cvrw", w_conv[:, :, row_tap, col_tap], window)
    return total


def weight_grad(grad, padded):
    height = grad.shape[2]
    breadth = grad.shape[3]
    taps = []
    for row_tap in range(3):
        for col_tap in range(3):
            window = padded[:, :, row_tap : row_tap + height, col_tap : col_tap + breadth]
            taps.append(product("ovrw,cvrw->oc", grad, window))
    stacked = jnp.stack(taps, axis=2)
    return stacked.reshape(grad.shape[0], padded.shape[0], 3, 3)


def angular(mixed_in, grad_out, keep, gain, w_query, w_key, w_value, w_out, used):
    pixels, all_views, channels = mixed_in.shape
    scale = 1.0 / math.sqrt(channels)
    values = mixed_in.astype(jnp.float32)
    centred = values - jnp.mean(values, axis=2, keepdims=True)
    rstd = lax.rsqrt(jnp.mean(centred * centred, axis=2, keepdims=True) + 1e-05)
    normed = centred * rstd
    normal_in = (normed * gain[None, None, :]).astype(jnp.bfloat16)
    query = product("cd,pvc->pvd", w_query, normal_in).astype(jnp.bfloat16)
    key_proj = product("cd,pvc->pvd", w_key, normal_in).astype(jnp.bfloat16)
    value_proj = product("cd,pvc->pvd", w_value, normal_in).astype(jnp.bfloat16)
    scores = product("pvd,pud->pvu", query, key_proj) * scale
    scores = jnp.where(keep[None, None, :used] > 0, scores, -1e30)
    highest = jnp.max(scores, axis=2, keepdims=True)
    expo = jnp.exp(scores - highest)
    probs = expo / jnp.sum(expo, axis=2, keepdims=True)
    probs_b = probs.astype(jnp.bfloat16)
    attended = product("pvu,pud->pvd", probs_b, value_proj).astype(jnp.bfloat16)
    output = (values + product("dc,pvd->pvc", w_out, attended)).astype(jnp.bfloat16)
    d_attended = product("dc,pvc->pvd", w_out, grad_out).astype(jnp.bfloat16)
    g_out = product("pvd,pvc->dc", attended, grad_out)
    d_probs = product("pvd,pud->pvu", d_attended, value_proj)
    d_value = product("pvu,pvd->pud", probs_b, d_attended).astype(jnp.bfloat16)
    inner = jnp.sum(probs * d_probs, axis=2, keepdims=True)
    d_scores = (probs * (d_probs - inner) * scale).astype(jnp.bfloat16)
    d_query = product("pvu,pud->pvd", d_scores, key_proj).astype(jnp.bfloat16)
    d_key = product("pvu,pvd->pud", d_scores, query).astype(jnp.bfloat16)
    g_query = product("pvc,pvd->cd", normal_in, d_query)
    g_key = product("pvc,pvd->cd", normal_in, d_key)
    g_value = product("pvc,pvd->cd", normal_in, d_value)
    d_normal = (
        product("cd,pvd->pvc", w_query, d_query)
        + product("cd,pvd->pvc", w_key, d_key)
        + product("cd,pvd->pvc", w_value, d_value)
    )
    g_gain = jnp.sum(d_normal * normed, axis=(0, 1))
    scaled = d_normal * gain[None, None, :]
    back = (
        scaled
        - jnp.mean(scaled, axis=2, keepdims=True)
        - normed * jnp.mean(scaled * normed, axis=2, keepdims=True)
    )
    d_spatial = (grad_out.astype(jnp.float32) + back * rstd).astype(jnp.bfloat16)
    return (output, d_spatial, (g_gain, g_query, g_key, g_value, g_out))


def angular_rows(spatial, cotangent, keep, gain, w_query, w_key, w_value, w_out, used):

    def row_pass(pair):
        return angular(pair[0], pair[1], keep, gain, w_query, w_key, w_value, w_out, used)

    spatial_last = jnp.transpose(spatial, (2, 3, 1, 0))
    cotangent_last = jnp.transpose(cotangent, (2, 3, 1, 0))
    out_rows, grad_rows, grads = lax.map(row_pass, (spatial_last, cotangent_last))
    summed = tuple((jnp.sum(item, axis=0) for item in grads))
    return (jnp.transpose(out_rows, (3, 2, 0, 1)), jnp.transpose(grad_rows, (3, 2, 0, 1)), summed)


def body(inputs, cotangent, keep, w_conv, gain, w_query, w_key, w_value, w_out):
    channels, view_dev, row_dev, width = inputs.shape
    blocks = lax.axis_size("view")
    breadth = width // blocks
    all_views = view_dev * blocks
    padded = with_halo(inputs, (("row", 2),), 1)
    padded = jnp.pad(padded, ((0, 0), (0, 0), (0, 0), (1, 1)))
    spatial = (inputs.astype(jnp.float32) + convolve(padded, w_conv)).astype(jnp.bfloat16)
    moved = lax.all_to_all(
        spatial.reshape(channels, view_dev, row_dev, blocks, breadth),
        "view",
        split_axis=3,
        concat_axis=1,
        tiled=True,
    )
    moved = moved.reshape(channels, all_views, row_dev, breadth)
    output, d_spatial, grads = angular_rows(
        moved, cotangent, keep, gain, w_query, w_key, w_value, w_out, all_views
    )
    returned = lax.all_to_all(
        d_spatial.reshape(channels, all_views, row_dev, 1, breadth),
        "view",
        split_axis=1,
        concat_axis=3,
        tiled=True,
    )
    returned = returned.reshape(channels, view_dev, row_dev, width)
    grad_pad = with_halo(returned, (("row", 2),), 1)
    grad_pad = jnp.pad(grad_pad, ((0, 0), (0, 0), (0, 0), (1, 1)))
    d_input = (returned.astype(jnp.float32) + input_grad(grad_pad, w_conv)).astype(jnp.bfloat16)
    g_conv = weight_grad(returned, padded)
    g_gain, g_query, g_key, g_value, g_out = grads
    g_conv, g_gain, g_query, g_key, g_value, g_out = lax.psum(
        (g_conv, g_gain, g_query, g_key, g_value, g_out), ("view", "row")
    )
    return (output, d_input, g_conv, g_gain, g_query, g_key, g_value, g_out)


def solution(mesh):
    placed = (
        P(None, "view", ("groups", "row"), None),
        P(None, None, ("groups", "row"), "view"),
        P("groups"),
        P(),
        P(),
        P(),
        P(),
        P(),
        P(),
    )
    return jax.shard_map(
        body,
        mesh=mesh,
        in_specs=placed,
        out_specs=(
            P(None, None, ("groups", "row"), "view"),
            P(None, "view", ("groups", "row"), None),
            P("groups", None, None, None),
            P("groups"),
            P("groups", None),
            P("groups", None),
            P("groups", None),
            P("groups", None),
        ),
        check_vma=False,
    )
```

profile of v0, /device:TPU:0, one launch (start us, length us, event | category | flops | bytes accessed | tf_op | source)
XLA Modules:
  0.0 311.2 jit_solution(1073874773569292355)
XLA Ops:
  8.4 2.4 collective-permute-start
  13.2 3.2 %collective-permute-done.1 = bf16[64,73,1,16]{1,0,3,2:T(8,128)(2,1)S(1)} collective-permute-done((bf16[64,73,1,16]{1,0,3,2:T(8,128)(2,1)S(1)}, bf16[64,73,1,16]{1,0,3,2:T(8,128)(2,1)S(1)}, u32[]{:S(2)}, u32[]{:S(2)}) %collective-permute-start.1) | collective-permute-done | bytes 149536 | tf_op jit(solution)/shard_map/ppermute | solution.py:18
  20.0 5.0 %all-to-all-start = ((bf16[64,73,2,4,4]{1,0,4,2,3:T(8,128)(2,1)}), bf16[64,73,2,4,4]{1,0,4,2,3:T(8,128)(2,1)S(1)}, u32[]{:S(2)}, u32[]{:S(2)}) async-start(bf16[64,73,2,4,4]{1,0,4,2,3:T(8,128)(2,1)} %copy.93), calls=%async_computation | async-start | bytes 1048576 | tf_op jit(solution)/shard_map/all_to_all | solution.py:131
  25.1 12.3 %all-to-all-done = bf16[64,73,2,4,4]{1,0,4,2,3:T(8,128)(2,1)S(1)} async-done(((bf16[64,73,2,4,4]{1,0,4,2,3:T(8,128)(2,1)}), bf16[64,73,2,4,4]{1,0,4,2,3:T(8,128)(2,1)S(1)}, u32[]{:S(2)}, u32[]{:S(2)}) %all-to-all-start) | async-done | bytes 299040 | tf_op jit(solution)/shard_map/all_to_all | solution.py:131
  38.2 56.6 %while.22 = (s32[]{:T(128)}, bf16[2,4,292,64]{2,1,0,3:T(4,128)(2,1)}, bf16[2,4,292,64]{2,3,1,0:T(8,128)(2,1)}, f32[2,64]{1,0:T(2,128)}, f32[2,64,64]{2,1,0:T(8,1...) while((s32[]{:T(128)}, ...), condition=%wide.region_9.10_spmd, body=%wide.region_0.9_spmd.sunk | while | flops 399432576 | bytes 35407752 | solution.py:118
  41.3 1.6 convolution_convert_fusion.12
  42.9 3.1 %fusion.288 = (f32[4,292]{1,0:T(4,128)S(1)}, f32[4,292,292]{1,2,0:T(8,128)}) fusion(pred[292]{0:T(512)(128)(4,1)S(1)} %broadcast_compare_fusion.2, bf16[4,292,64]{1,2,0:T(8,128)(2,1)} %convolution_convert_fusion.12, bf16[64,64]{1,0:T(8,128)(2,1)S(1)} %copy-done.17, f32[64]{0:T(128)} %get-tuple-element.425, f32[4,292]{1,0:T(4,128)S(1)} %add_rsqrt_fusion.2, ...), kind=kOutput, calls=%fused_computation.193.clone.1 | convolution fusion | flops 55036452 | bytes 1744452 | tf_op jit(solution)/shard_map/while/body/eval_jaxpr/sub | solution.py:79
  46.0 3.5 %fusion.293 = bf16[4,292,64]{1,2,0:T(8,128)(2,1)} fusion(f32[4,292,292]{1,2,0:T(8,128)S(1)} %fusion.290, f32[4,292,292]{1,2,0:T(8,128)} %get-tuple-element.288, f32[4,292]{1,0:T(4,128)S(1)} %get-tuple-element.289, bf16[64,64]{1,0:T(8,128)(2,1)S(1)} %copy-done.17, f32[64]{0:T(128)} %get-tuple-element.425, f32[4,292]{1,0:T(4,128)S(1)} %add_rsqrt_fusion.2, ...), kind=kOutput, calls=%fused_computation.14.clone.1 | convolution fusion | flops 56135540 | bytes 7662592 | tf_op jit(solution)/shard_map/while/body/eval_jaxpr/pvu,pvd->pud/dot_general | solution.py:26
  49.6 3.5 %fusion.291 = bf16[4,292,64]{1,2,0:T(8,128)(2,1)} fusion(bf16[4,292,64]{1,2,0:T(8,128)(2,1)} %convolution_convert_fusion.12, f32[4,292,292]{1,2,0:T(8,128)S(1)} %fusion.290, f32[4,292,292]{1,2,0:T(8,128)} %get-tuple-element.288, f32[4,292]{1,0:T(4,128)S(1)} %get-tuple-element.289), kind=kOutput, calls=%fused_computation.13.clone.1 | convolution fusion | flops 46118772 | bytes 3032128 | tf_op jit(solution)/shard_map/while/body/eval_jaxpr/pvu,pud->pvd/dot_general | solution.py:26
  55.3 2.0 convolution_convert_fusion.15
  62.5 1.9 convolution_convert_fusion.13
  69.6 1.6 convolution_convert_fusion.12
  71.2 3.1 %fusion.288 = (f32[4,292]{1,0:T(4,128)S(1)}, f32[4,292,292]{1,2,0:T(8,128)}) fusion(pred[292]{0:T(512)(128)(4,1)S(1)} %broadcast_compare_fusion.2, bf16[4,292,64]{1,2,0:T(8,128)(2,1)} %convolution_convert_fusion.12, bf16[64,64]{1,0:T(8,128)(2,1)S(1)} %copy-done.17, f32[64]{0:T(128)} %get-tuple-element.425, f32[4,292]{1,0:T(4,128)S(1)} %add_rsqrt_fusion.2, ...), kind=kOutput, calls=%fused_computation.193.clone.1 | convolution fusion | flops 55036452 | bytes 1744452 | tf_op jit(solution)/shard_map/while/body/eval_jaxpr/sub | solution.py:79
  74.3 3.5 %fusion.293 = bf16[4,292,64]{1,2,0:T(8,128)(2,1)} fusion(f32[4,292,292]{1,2,0:T(8,128)S(1)} %fusion.290, f32[4,292,292]{1,2,0:T(8,128)} %get-tuple-element.288, f32[4,292]{1,0:T(4,128)S(1)} %get-tuple-element.289, bf16[64,64]{1,0:T(8,128)(2,1)S(1)} %copy-done.17, f32[64]{0:T(128)} %get-tuple-element.425, f32[4,292]{1,0:T(4,128)S(1)} %add_rsqrt_fusion.2, ...), kind=kOutput, calls=%fused_computation.14.clone.1 | convolution fusion | flops 56135540 | bytes 7662592 | tf_op jit(solution)/shard_map/while/body/eval_jaxpr/pvu,pvd->pud/dot_general | solution.py:26
  77.9 3.5 %fusion.291 = bf16[4,292,64]{1,2,0:T(8,128)(2,1)} fusion(bf16[4,292,64]{1,2,0:T(8,128)(2,1)} %convolution_convert_fusion.12, f32[4,292,292]{1,2,0:T(8,128)S(1)} %fusion.290, f32[4,292,292]{1,2,0:T(8,128)} %get-tuple-element.288, f32[4,292]{1,0:T(4,128)S(1)} %get-tuple-element.289), kind=kOutput, calls=%fused_computation.13.clone.1 | convolution fusion | flops 46118772 | bytes 3032128 | tf_op jit(solution)/shard_map/while/body/eval_jaxpr/pvu,pud->pvd/dot_general | solution.py:26
  83.6 2.0 convolution_convert_fusion.15
  90.8 1.9 convolution_convert_fusion.13
  94.8 1.6 copy.97
  97.8 5.2 %all-to-all-start.1 = ((bf16[4,2,18688]{2,1,0:T(2,128)(2,1)}), bf16[4,2,18688]{2,1,0:T(2,128)(2,1)S(1)}, u32[]{:S(2)}, u32[]{:S(2)}) async-start(bf16[4,2,18688]{2,1,0:T(2,128)(2,1)} %reshape.106), calls=%async_computation.1 | async-start | bytes 598016 | tf_op jit(solution)/shard_map/all_to_all | solution.py:142
  106.3 6.2 %all-to-all-done.1 = bf16[4,2,18688]{2,1,0:T(2,128)(2,1)S(1)} async-done(((bf16[4,2,18688]{2,1,0:T(2,128)(2,1)}), bf16[4,2,18688]{2,1,0:T(2,128)(2,1)S(1)}, u32[]{:S(2)}, u32[]{:S(2)}) %all-to-all-start.1) | async-done | bytes 299040 | tf_op jit(solution)/shard_map/all_to_all | solution.py:142
  118.7 4.0 %collective-permute-start.2 = (bf16[64,73,1,16]{1,0,3,2:T(8,128)(2,1)S(1)}, bf16[64,73,1,16]{1,0,3,2:T(8,128)(2,1)S(1)}, u32[]{:S(2)}, u32[]{:S(2)}) collective-permute-start(bf16[64,73,1,16]{1,0,3,2:T(8,128)(2,1)S(1)} %get-tuple-element.172), channel_id=1, source_target_pairs={{0,1},{1,2},{2,3},{4,5},{5,6},{6,7},{8,9},{9,10},{10,11},{12,13},{... | collective-permute-start | bytes 448520 | tf_op jit(solution)/shard_map/ppermute | solution.py:16
  127.6 71.4 %all-reduce.8.cloned.1.call-done = (f32[64]{0:T(128)}, f32[64,64]{1,0:T(8,128)}, f32[64,64]{1,0:T(8,128)}, f32[64,64]{1,0:T(8,128)}, f32[64,64]{1,0:T(8,128)}) async-done(((f32[64]{0:T(128)}, f32[64,64]{1,0:T(8,128)}, f32[64,64]{1,0:T(8,128)}, f32[64,64]{1,0:T(8,128)}, f32[64,64]{1,0:T(8,128)}), (f32[64]{0:T(128)}, f32[64,64]{1,0:T(8,128)}, f32[64,64]{1,0:T(8,128)}, f32[64,64]{1,0:T(8,128)}, ...) | async-done | bytes 65808 | tf_op jit(solution)/shard_map/psum | solution.py:155
  199.0 97.0 %all-reduce.6.cloned.1.call-done = f32[64,64,3,3]{1,0,3,2:T(8,128)} async-done(((f32[64,64,3,3]{1,0,3,2:T(8,128)}), f32[64,64,3,3]{1,0,3,2:T(8,128)}) %all-reduce.6.cloned.1.call-update) | async-done | bytes 147472 | tf_op jit(solution)/shard_map/psum | solution.py:155
  296.0 1.7 copy.226
  (251 shorter events, 54.5 us)
Async XLA Ops:
  8.4 4.1 %collective-permute-start = (bf16[64,73,1,16]{1,0,3,2:T(8,128)(2,1)S(1)}, bf16[64,73,1,16]{1,0,3,2:T(8,128)(2,1)S(1)}, u32[]{:S(2)}, u32[]{:S(2)}) collective-permute-start(bf16[64,73,1,16]{1,0,3,2:T(8,128)(2,1)S(1)} %copy.172), channel_id=1, source_target_pairs={{0,1},{1,2},{2,3},{4,5},{5,6},{6,7},{8,9},{9,10},{10,11},{12,13},{... | collective-permute-start | bytes 448520 | tf_op jit(solution)/shard_map/ppermute | solution.py:16
  10.9 5.5 %collective-permute-start.1 = (bf16[64,73,1,16]{1,0,3,2:T(8,128)(2,1)S(1)}, bf16[64,73,1,16]{1,0,3,2:T(8,128)(2,1)S(1)}, u32[]{:S(2)}, u32[]{:S(2)}) collective-permute-start(bf16[64,73,1,16]{1,0,3,2:T(8,128)(2,1)S(1)} %copy.173), channel_id=1, source_target_pairs={{1,0},{2,1},{3,2},{5,4},{6,5},{7,6},{9,8},{10,9},{11,10},{13,12},{... | collective-permute-start | bytes 448520 | tf_op jit(solution)/shard_map/ppermute | solution.py:18
  19.1 5.9 %copy-start.18 = (bf16[64,292,2,4]{1,3,2,0:T(4,128)(2,1)S(1)}, bf16[64,292,2,4]{1,3,2,0:T(4,128)(2,1)}, u32[]{:S(2)}) copy-start(bf16[64,292,2,4]{1,3,2,0:T(4,128)(2,1)} %param.12) | copy-start | bytes 897028
  20.0 18.2 %copy-start.12 = (bf16[64,64]{1,0:T(8,128)(2,1)S(1)}, bf16[64,64]{1,0:T(8,128)(2,1)}, u32[]{:S(2)}) copy-start(bf16[64,64]{1,0:T(8,128)(2,1)} %param.19) | copy-start | bytes 24580
  20.0 18.2 %copy-start.15 = (bf16[64,64]{1,0:T(8,128)(2,1)S(1)}, bf16[64,64]{1,0:T(8,128)(2,1)}, u32[]{:S(2)}) copy-start(bf16[64,64]{1,0:T(8,128)(2,1)} %param.18) | copy-start | bytes 24580
  20.0 18.2 %copy-start.34 = (f32[64]{0:T(128)S(1)}, f32[64]{0:T(128)}, u32[]{:S(2)}) copy-start(f32[64]{0:T(128)} %param.15) | copy-start | bytes 772
  20.0 17.4 %all-to-all-start = ((bf16[64,73,2,4,4]{1,0,4,2,3:T(8,128)(2,1)}), bf16[64,73,2,4,4]{1,0,4,2,3:T(8,128)(2,1)S(1)}, u32[]{:S(2)}, u32[]{:S(2)}) async-start(bf16[64,73,2,4,4]{1,0,4,2,3:T(8,128)(2,1)} %copy.93), calls=%async_computation | async-start | bytes 1048576 | tf_op jit(solution)/shard_map/all_to_all | solution.py:131
  46.0 9.2 %copy-start.42 = (f32[4,292]{1,0:T(4,128)}, f32[4,292]{1,0:T(4,128)S(1)}, u32[]{:S(2)}) copy-start(f32[4,292]{1,0:T(4,128)S(1)} %get-tuple-element.289) | copy-start | bytes 14020 | tf_op jit(solution)/shard_map/while
  57.4 5.1 %copy-start.5 = (bf16[4,292,64]{1,2,0:T(8,128)(2,1)S(1)}, bf16[4,292,64]{1,2,0:T(8,128)(2,1)}, u32[]{:S(2)}) copy-start(bf16[4,292,64]{1,2,0:T(8,128)(2,1)} %copy-done.4) | copy-start | bytes 448516 | tf_op jit(solution)/shard_map/while
  57.4 5.1 %copy-start.43 = (f32[4,292]{1,0:T(4,128)S(1)}, f32[4,292]{1,0:T(4,128)}, u32[]{:S(2)}) copy-start(f32[4,292]{1,0:T(4,128)} %copy-done.42) | copy-start | bytes 14020 | tf_op jit(solution)/shard_map/while
  74.3 9.2 %copy-start.42 = (f32[4,292]{1,0:T(4,128)}, f32[4,292]{1,0:T(4,128)S(1)}, u32[]{:S(2)}) copy-start(f32[4,292]{1,0:T(4,128)S(1)} %get-tuple-element.289) | copy-start | bytes 14020 | tf_op jit(solution)/shard_map/while
  85.7 5.1 %copy-start.5 = (bf16[4,292,64]{1,2,0:T(8,128)(2,1)S(1)}, bf16[4,292,64]{1,2,0:T(8,128)(2,1)}, u32[]{:S(2)}) copy-start(bf16[4,292,64]{1,2,0:T(8,128)(2,1)} %copy-done.4) | copy-start | bytes 448516 | tf_op jit(solution)/shard_map/while
  85.7 5.1 %copy-start.43 = (f32[4,292]{1,0:T(4,128)S(1)}, f32[4,292]{1,0:T(4,128)}, u32[]{:S(2)}) copy-start(f32[4,292]{1,0:T(4,128)} %copy-done.42) | copy-start | bytes 14020 | tf_op jit(solution)/shard_map/while
  94.8 8.2 %copy-start.27 = (f32[2,64,64]{2,1,0:T(8,128)S(1)}, f32[2,64,64]{2,1,0:T(8,128)}, u32[]{:S(2)}) copy-start(f32[2,64,64]{2,1,0:T(8,128)} %get-tuple-element.410) | copy-start | bytes 98308
  94.8 8.8 %copy-start.30 = (f32[2,64,64]{2,1,0:T(8,128)S(1)}, f32[2,64,64]{2,1,0:T(8,128)}, u32[]{:S(2)}) copy-start(f32[2,64,64]{2,1,0:T(8,128)} %get-tuple-element.411) | copy-start | bytes 98308
  94.8 9.4 %copy-start.33 = (f32[2,64,64]{2,1,0:T(8,128)S(1)}, f32[2,64,64]{2,1,0:T(8,128)}, u32[]{:S(2)}) copy-start(f32[2,64,64]{2,1,0:T(8,128)} %get-tuple-element.412) | copy-start | bytes 98308
  94.8 10.1 %copy-start.24 = (f32[2,64,64]{2,1,0:T(8,128)S(1)}, f32[2,64,64]{2,1,0:T(8,128)}, u32[]{:S(2)}) copy-start(f32[2,64,64]{2,1,0:T(8,128)} %get-tuple-element.413) | copy-start | bytes 98308
  94.8 10.7 %copy-start.39 = (f32[2,64]{1,0:T(2,128)S(1)}, f32[2,64]{1,0:T(2,128)}, u32[]{:S(2)}) copy-start(f32[2,64]{1,0:T(2,128)} %get-tuple-element.409) | copy-start | bytes 1540
  97.8 14.7 %all-to-all-start.1 = ((bf16[4,2,18688]{2,1,0:T(2,128)(2,1)}), bf16[4,2,18688]{2,1,0:T(2,128)(2,1)S(1)}, u32[]{:S(2)}, u32[]{:S(2)}) async-start(bf16[4,2,18688]{2,1,0:T(2,128)(2,1)} %reshape.106), calls=%async_computation.1 | async-start | bytes 598016 | tf_op jit(solution)/shard_map/all_to_all | solution.py:142
  103.0 96.1 %all-reduce.8.cloned.1.call-start = ((), (), s32[]{:S(2)}) async-start(), calls=%async_computation.3 | async-start | bytes 263168 | tf_op jit(solution)/shard_map/psum | solution.py:155
  106.0 190.0 %all-reduce.6.cloned.1.call-start = ((), (), s32[]{:S(2)}) async-start(), calls=%async_computation.2 | async-start | bytes 589824 | tf_op jit(solution)/shard_map/psum | solution.py:155
  117.4 5.3 %copy-start.21 = (f32[64,64,9]{1,0,2:T(8,128)}, f32[64,64,9]{1,0,2:T(8,128)S(1)}, u32[]{:S(2)}) copy-start(f32[64,64,9]{1,0,2:T(8,128)S(1)} %fusion.104) | copy-start | bytes 442372
  117.4 5.6 %collective-permute-start.3 = (bf16[64,73,1,16]{1,0,3,2:T(8,128)(2,1)S(1)}, bf16[64,73,1,16]{1,0,3,2:T(8,128)(2,1)S(1)}, u32[]{:S(2)}, u32[]{:S(2)}) collective-permute-start(bf16[64,73,1,16]{1,0,3,2:T(8,128)(2,1)S(1)} %get-tuple-element.173), channel_id=1, source_target_pairs={{1,0},{2,1},{3,2},{5,4},{6,5},{7,6},{9,8},{10,9},{11,10},{13,12},{... | collective-permute-start | bytes 448520 | tf_op jit(solution)/shard_map/ppermute | solution.py:18
  118.7 5.1 %collective-permute-start.2 = (bf16[64,73,1,16]{1,0,3,2:T(8,128)(2,1)S(1)}, bf16[64,73,1,16]{1,0,3,2:T(8,128)(2,1)S(1)}, u32[]{:S(2)}, u32[]{:S(2)}) collective-permute-start(bf16[64,73,1,16]{1,0,3,2:T(8,128)(2,1)S(1)} %get-tuple-element.172), channel_id=1, source_target_pairs={{0,1},{1,2},{2,3},{4,5},{5,6},{6,7},{8,9},{9,10},{10,11},{12,13},{... | collective-permute-start | bytes 448520 | tf_op jit(solution)/shard_map/ppermute | solution.py:16
  (55 other events, 161.9 us)
Sparse Core Ops, SparseCore 0:
  108.4 90.5 all-reduce.7
  203.0 93.0 all-reduce.5
where the time goes:
time: 313 us; the launch traced here: 311 us
  waiting for transfers between devices  191 us (61%)
  matrix products  58.5 us (19%)
  local copies, waits for them, and re-layouts  22.2 us (7%)
  starting transfers between devices  19.4 us (6%)
  between operations  14.6 us (5%)
  other arithmetic  5.07 us (2%)
    psum x2, waiting for transfers between devices, body(): lax.psum((g_conv, g_gain, g_query, g_key, g_value, g_out), ('view', 'row'))  168 us
    dot_general x59, matrix products, product(): return jnp.einsum(form, left, right, preferred_element_type=jnp.float32)  52.2 us
    unnamed x48, local copies, waits for them, and re-layouts  12.6 us
    all_to_all x1, waiting for transfers between devices, body(): lax.all_to_all(spatial.reshape(channels, view_dev, row_dev, blocks, bread...  12.3 us
    ppermute x2, starting transfers between devices, with_halo(): lax.ppermute(tail, axis, [(i, (i + 1) % count) for i in range(ends)])  6.37 us
  transfers between devices with their start and end apart: 8, of which 6 were waited for; matrix products, arithmetic and copies ran while one was open for 4% of the time, Pallas kernels for 0%

commit v1 on v0

--- a/solution.py
+++ b/solution.py
@@ -3,6 +3,29 @@
 import jax.numpy as jnp
 from jax import lax
 from jax.sharding import PartitionSpec as P
+
+
+def split_up(value, dim, size):
+    before, after = (value.shape[:dim], value.shape[dim + 1 :])
+    return jnp.moveaxis(value.reshape(*before, size, -1, *after), dim, 0)
+
+
+def in_order(blocks, dim):
+    dims = list(blocks.shape[1:])
+    dims[dim] *= blocks.shape[0]
+    return jnp.moveaxis(blocks, 0, dim).reshape(dims)
+
+
+def exchange_directly(array, axis, split_dim, concat_dim):
+    size, index = (lax.axis_size(axis), lax.axis_index(axis))
+    blocks = split_up(array, split_dim, size)
+    out = blocks
+    for step in range(1, size):
+        target, source = ((index + step) % size, (index - step) % size)
+        sent = lax.dynamic_index_in_dim(blocks, target, 0)
+        other = lax.ppermute(sent, axis, [(i, (i + step) % size) for i in range(size)])
+        out = lax.dynamic_update_slice_in_dim(out, other, source, axis=0)
+    return in_order(out, concat_dim)
 
 
 def with_halo(cells, sides, width):
@@ -128,12 +151,8 @@
     padded = with_halo(inputs, (("row", 2),), 1)
     padded = jnp.pad(padded, ((0, 0), (0, 0), (0, 0), (1, 1)))
     spatial = (inputs.astype(jnp.float32) + convolve(padded, w_conv)).astype(jnp.bfloat16)
-    moved = lax.all_to_all(
-        spatial.reshape(channels, view_dev, row_dev, blocks, breadth),
-        "view",
-        split_axis=3,
-        concat_axis=1,
-        tiled=True,
+    moved = exchange_directly(
+        spatial.reshape(channels, view_dev, row_dev, blocks, breadth), "view", 3, 1
     )
     moved = moved.reshape(channels, all_views, row_dev, breadth)
     output, d_spatial, grads = angular_rows(

time: 313 us -> 298 us (0.952)
  waiting for transfers between devices: 191 us -> 184 us
  matrix products: 58.5 us -> 52.7 us
    all_to_all x1 -> x0, waiting for transfers between devices: 12.3 us -> none  [body(): lax.all_to_all(spatial.reshape(channels, view_dev, row_dev, blocks, bread...]
    ppermute x0 -> x3, waiting for transfers between devices: none -> 6.3 us  [exchange_directly(): lax.ppermute(sent, axis, [(i, (i + step) % size) for i in range(size)])]
    dot_general x59, matrix products: 52.2 us -> 46.5 us  [product(): return jnp.einsum(form, left, right, preferred_element_type=jnp.float32)]
    ppermute x0 -> x3, starting transfers between devices: none -> 5.63 us  [exchange_directly(): lax.ppermute(sent, axis, [(i, (i + step) % size) for i in range(size)])]
    all_to_all x1 -> x0, starting transfers between devices: 5 us -> none  [body(): lax.all_to_all(spatial.reshape(channels, view_dev, row_dev, blocks, bread...]
    unnamed x48 -> x50, local copies, waits for them, and re-layouts: 12.6 us -> 12.5 us
  transfers between devices with their start and end apart: 8 -> 10, of which waited for: 6 -> 8; matrix products, arithmetic and copies ran while one was open for 4% -> 4% of each run, Pallas kernels for 0% -> 0%
where the time goes in v1:
time: 298 us; the launch traced here: 297 us
  waiting for transfers between devices  184 us (62%)
  matrix products  52.7 us (18%)
  local copies, waits for them, and re-layouts  20.3 us (7%)
  starting transfers between devices  20 us (7%)
  between operations  14.7 us (5%)
  other arithmetic  4.6 us (2%)
    psum x2, waiting for transfers between devices, body(): lax.psum((g_conv, g_gain, g_query, g_key, g_value, g_out), ('view', 'row'))  169 us
    dot_general x59, matrix products, product(): return jnp.einsum(form, left, right, preferred_element_type=jnp.float32)  46.5 us
    unnamed x50, local copies, waits for them, and re-layouts  12.5 us
    ppermute x2, starting transfers between devices, with_halo(): lax.ppermute(tail, axis, [(i, (i + 1) % count) for i in range(ends)])  6.59 us
    ppermute x3, waiting for transfers between devices, exchange_directly(): lax.ppermute(sent, axis, [(i, (i + step) % size) for i in range(size)])  6.3 us
    sub x2, matrix products, angular(): expo = jnp.exp(scores - highest)  6.21 us
  transfers between devices with their start and end apart: 10, of which 8 were waited for; matrix products, arithmetic and copies ran while one was open for 4% of the time, Pallas kernels for 0%

profile of v1, /device:TPU:0, one launch (start us, length us, event | category | flops | bytes accessed | tf_op | source)
XLA Modules:
  0.0 297.1 jit_solution(12554850316800547743)
XLA Ops:
  8.4 2.4 collective-permute-start
  13.2 3.2 %collective-permute-done.1 = bf16[64,73,1,16]{1,0,3,2:T(8,128)(2,1)S(1)} collective-permute-done((bf16[64,73,1,16]{1,0,3,2:T(8,128)(2,1)S(1)}, bf16[64,73,1,16]{1,0,3,2:T(8,128)(2,1)S(1)}, u32[]{:S(2)}, u32[]{:S(2)}) %collective-permute-start.1) | collective-permute-done | bytes 149536 | tf_op jit(solution)/shard_map/ppermute | solution.py:41
  19.2 1.6 collective-permute-start.2
  21.0 2.7 collective-permute-start.3
  26.0 3.4 %collective-permute-done.3 = bf16[1,64,73,2,1,4]{2,1,5,0,3,4:T(8,128)(2,1)S(1)} collective-permute-done((bf16[1,64,73,2,1,4]{2,1,5,0,3,4:T(8,128)(2,1)S(1)}, bf16[1,64,73,2,1,4]{2,1,5,0,3,4:T(8,128)(2,1)S(1)}, u32[]{:S(2)}, u32[]{:S(2)}) %collective-permute-start.3) | collective-permute-done | bytes 74784 | tf_op jit(solution)/shard_map/ppermute | solution.py:26
  29.4 1.9 collective-permute-done.4
  32.2 48.1 %while.22 = (s32[]{:T(128)}, bf16[2,4,292,64]{2,1,0,3:T(4,128)(2,1)}, bf16[2,4,292,64]{2,3,1,0:T(8,128)(2,1)}, f32[2,64]{1,0:T(2,128)S(1)}, f32[2,64,64]{2,1,0:T...) while((s32[]{:T(128)}, ...), condition=%wide.region_9.10_spmd, body=%wide.region_0.9_spmd.sunk | while | flops 399432576 | bytes 35000580 | solution.py:141
  36.3 3.1 %fusion.288 = (f32[4,292]{1,0:T(4,128)S(1)}, f32[4,292,292]{1,2,0:T(8,128)}) fusion(pred[292]{0:T(512)(128)(4,1)S(1)} %broadcast_compare_fusion.2, bf16[4,292,64]{1,2,0:T(8,128)(2,1)} %convolution_convert_fusion.12, bf16[64,64]{1,0:T(8,128)(2,1)S(1)} %get-tuple-element.338, f32[64]{0:T(128)S(1)} %get-tuple-element.337, ...), kind=kOutput, calls=%fused_computation.199.clone.1 | convolution fusion | flops 55036452 | bytes 1744708 | tf_op jit(solution)/shard_map/while/body/eval_jaxpr/sub | solution.py:102
  39.4 3.5 %fusion.293 = bf16[4,292,64]{1,2,0:T(8,128)(2,1)} fusion(f32[4,292,292]{1,2,0:T(8,128)S(1)} %fusion.290, f32[4,292,292]{1,2,0:T(8,128)} %get-tuple-element.283, f32[4,292]{1,0:T(4,128)S(1)} %get-tuple-element.284, bf16[64,64]{1,0:T(8,128)(2,1)S(1)} %get-tuple-element.338, f32[64]{0:T(128)S(1)} %get-tuple-element.337, ...), kind=kOutput, calls=%fused_computation.14.clone.1 | convolution fusion | flops 56135540 | bytes 7662592 | tf_op jit(solution)/shard_map/while/body/eval_jaxpr/pvu,pvd->pud/dot_general | solution.py:49
  42.9 3.5 %fusion.291 = bf16[4,292,64]{1,2,0:T(8,128)(2,1)} fusion(bf16[4,292,64]{1,2,0:T(8,128)(2,1)} %convolution_convert_fusion.12, f32[4,292,292]{1,2,0:T(8,128)S(1)} %fusion.290, f32[4,292,292]{1,2,0:T(8,128)} %get-tuple-element.283, f32[4,292]{1,0:T(4,128)S(1)} %get-tuple-element.284), kind=kOutput, calls=%fused_computation.13.clone.1 | convolution fusion | flops 46118772 | bytes 3032128 | tf_op jit(solution)/shard_map/while/body/eval_jaxpr/pvu,pud->pvd/dot_general | solution.py:49
  48.7 2.0 convolution_convert_fusion.15
  53.0 1.9 convolution_convert_fusion.13
  60.3 3.1 %fusion.288 = (f32[4,292]{1,0:T(4,128)S(1)}, f32[4,292,292]{1,2,0:T(8,128)}) fusion(pred[292]{0:T(512)(128)(4,1)S(1)} %broadcast_compare_fusion.2, bf16[4,292,64]{1,2,0:T(8,128)(2,1)} %convolution_convert_fusion.12, bf16[64,64]{1,0:T(8,128)(2,1)S(1)} %get-tuple-element.338, f32[64]{0:T(128)S(1)} %get-tuple-element.337, ...), kind=kOutput, calls=%fused_computation.199.clone.1 | convolution fusion | flops 55036452 | bytes 1744708 | tf_op jit(solution)/shard_map/while/body/eval_jaxpr/sub | solution.py:102
  63.4 3.5 %fusion.293 = bf16[4,292,64]{1,2,0:T(8,128)(2,1)} fusion(f32[4,292,292]{1,2,0:T(8,128)S(1)} %fusion.290, f32[4,292,292]{1,2,0:T(8,128)} %get-tuple-element.283, f32[4,292]{1,0:T(4,128)S(1)} %get-tuple-element.284, bf16[64,64]{1,0:T(8,128)(2,1)S(1)} %get-tuple-element.338, f32[64]{0:T(128)S(1)} %get-tuple-element.337, ...), kind=kOutput, calls=%fused_computation.14.clone.1 | convolution fusion | flops 56135540 | bytes 7662592 | tf_op jit(solution)/shard_map/while/body/eval_jaxpr/pvu,pvd->pud/dot_general | solution.py:49
  66.9 3.5 %fusion.291 = bf16[4,292,64]{1,2,0:T(8,128)(2,1)} fusion(bf16[4,292,64]{1,2,0:T(8,128)(2,1)} %convolution_convert_fusion.12, f32[4,292,292]{1,2,0:T(8,128)S(1)} %fusion.290, f32[4,292,292]{1,2,0:T(8,128)} %get-tuple-element.283, f32[4,292]{1,0:T(4,128)S(1)} %get-tuple-element.284), kind=kOutput, calls=%fused_computation.13.clone.1 | convolution fusion | flops 46118772 | bytes 3032128 | tf_op jit(solution)/shard_map/while/body/eval_jaxpr/pvu,pud->pvd/dot_general | solution.py:49
  72.7 2.0 convolution_convert_fusion.15
  77.1 1.9 convolution_convert_fusion.13
  80.3 1.6 copy.65
  83.2 5.0 %all-to-all-start = ((bf16[4,2,18688]{2,1,0:T(2,128)(2,1)}), bf16[4,2,18688]{2,1,0:T(2,128)(2,1)S(1)}, u32[]{:S(2)}, u32[]{:S(2)}) async-start(bf16[4,2,18688]{2,1,0:T(2,128)(2,1)} %reshape.100), calls=%async_computation | async-start | bytes 598016 | tf_op jit(solution)/shard_map/all_to_all | solution.py:161
  92.3 5.2 %all-to-all-done = bf16[4,2,18688]{2,1,0:T(2,128)(2,1)S(1)} async-done(((bf16[4,2,18688]{2,1,0:T(2,128)(2,1)}), bf16[4,2,18688]{2,1,0:T(2,128)(2,1)S(1)}, u32[]{:S(2)}, u32[]{:S(2)}) %all-to-all-start) | async-done | bytes 299040 | tf_op jit(solution)/shard_map/all_to_all | solution.py:161
  103.7 4.2 %collective-permute-start.5 = (bf16[64,73,1,16]{1,0,3,2:T(8,128)(2,1)S(1)}, bf16[64,73,1,16]{1,0,3,2:T(8,128)(2,1)S(1)}, u32[]{:S(2)}, u32[]{:S(2)}) collective-permute-start(bf16[64,73,1,16]{1,0,3,2:T(8,128)(2,1)S(1)} %get-tuple-element.164), channel_id=1, source_target_pairs={{0,1},{1,2},{2,3},{4,5},{5,6},{6,7},{8,9},{9,10},{10,11},{12,13},{... | collective-permute-start | bytes 448520 | tf_op jit(solution)/shard_map/ppermute | solution.py:39
  112.9 72.1 %all-reduce.8.cloned.1.call-done = (f32[64]{0:T(128)}, f32[64,64]{1,0:T(8,128)}, f32[64,64]{1,0:T(8,128)}, f32[64,64]{1,0:T(8,128)}, f32[64,64]{1,0:T(8,128)}) async-done(((f32[64]{0:T(128)}, f32[64,64]{1,0:T(8,128)}, f32[64,64]{1,0:T(8,128)}, f32[64,64]{1,0:T(8,128)}, f32[64,64]{1,0:T(8,128)}), (f32[64]{0:T(128)}, f32[64,64]{1,0:T(8,128)}, f32[64,64]{1,0:T(8,128)}, f32[64,64]{1,0:T(8,128)}, ...) | async-done | bytes 65808 | tf_op jit(solution)/shard_map/psum | solution.py:174
  185.0 97.0 %all-reduce.6.cloned.1.call-done = f32[64,64,3,3]{1,0,3,2:T(8,128)} async-done(((f32[64,64,3,3]{1,0,3,2:T(8,128)}), f32[64,64,3,3]{1,0,3,2:T(8,128)}) %all-reduce.6.cloned.1.call-update) | async-done | bytes 147472 | tf_op jit(solution)/shard_map/psum | solution.py:174
  282.0 1.7 copy.197
  (216 shorter events, 51.9 us)
Async XLA Ops:
  7.2 5.1 %copy-start.2 = (bf16[64,73,2,16]{1,3,2,0:T(8,128)(2,1)S(1)}, bf16[64,73,2,16]{1,3,2,0:T(8,128)(2,1)}, u32[]{:S(2)}) copy-start(bf16[64,73,2,16]{1,3,2,0:T(8,128)(2,1)} %param.11) | copy-start | bytes 897028
  7.2 5.1 %copy-start.13 = (bf16[64,64,3,3]{1,0,3,2:T(8,128)(2,1)S(1)}, bf16[64,64,3,3]{1,0,3,2:T(8,128)(2,1)}, u32[]{:S(2)}) copy-start(bf16[64,64,3,3]{1,0,3,2:T(8,128)(2,1)} %param.14) | copy-start | bytes 221188
  8.4 4.2 %collective-permute-start = (bf16[64,73,1,16]{1,0,3,2:T(8,128)(2,1)S(1)}, bf16[64,73,1,16]{1,0,3,2:T(8,128)(2,1)S(1)}, u32[]{:S(2)}, u32[]{:S(2)}) collective-permute-start(bf16[64,73,1,16]{1,0,3,2:T(8,128)(2,1)S(1)} %copy.140), channel_id=1, source_target_pairs={{0,1},{1,2},{2,3},{4,5},{5,6},{6,7},{8,9},{9,10},{10,11},{12,13},{... | collective-permute-start | bytes 448520 | tf_op jit(solution)/shard_map/ppermute | solution.py:39
  10.9 5.5 %collective-permute-start.1 = (bf16[64,73,1,16]{1,0,3,2:T(8,128)(2,1)S(1)}, bf16[64,73,1,16]{1,0,3,2:T(8,128)(2,1)S(1)}, u32[]{:S(2)}, u32[]{:S(2)}) collective-permute-start(bf16[64,73,1,16]{1,0,3,2:T(8,128)(2,1)S(1)} %copy.141), channel_id=1, source_target_pairs={{1,0},{2,1},{3,2},{5,4},{6,5},{7,6},{9,8},{10,9},{11,10},{13,12},{... | collective-permute-start | bytes 448520 | tf_op jit(solution)/shard_map/ppermute | solution.py:41
  19.2 6.9 %collective-permute-start.2 = (bf16[1,64,73,2,1,4]{2,1,5,0,3,4:T(8,128)(2,1)S(1)}, bf16[1,64,73,2,1,4]{2,1,5,0,3,4:T(8,128)(2,1)S(1)}, u32[]{:S(2)}, u32[]{:S(2)}) collective-permute-start(bf16[1,64,73,2,1,4]{2,1,5,0,3,4:T(8,128)(2,1)S(1)} %get-tuple-element.168), channel_id=1, source_target_pairs={{0,4},{4,8},{8,12},{12,0},{1,5},{5,9},{9,13},{13,1},{2,6},{6,10},{... | collective-permute-start | bytes 224264 | tf_op jit(solution)/shard_map/ppermute | solution.py:26
  20.8 11.4 %copy-start.12 = (bf16[64,64]{1,0:T(8,128)(2,1)S(1)}, bf16[64,64]{1,0:T(8,128)(2,1)}, u32[]{:S(2)}) copy-start(bf16[64,64]{1,0:T(8,128)(2,1)} %param.19) | copy-start | bytes 24580
  20.8 11.4 %copy-start.14 = (bf16[64,64]{1,0:T(8,128)(2,1)S(1)}, bf16[64,64]{1,0:T(8,128)(2,1)}, u32[]{:S(2)}) copy-start(bf16[64,64]{1,0:T(8,128)(2,1)} %param.17) | copy-start | bytes 24580
  20.8 11.4 %copy-start.15 = (bf16[64,64]{1,0:T(8,128)(2,1)S(1)}, bf16[64,64]{1,0:T(8,128)(2,1)}, u32[]{:S(2)}) copy-start(bf16[64,64]{1,0:T(8,128)(2,1)} %param.18) | copy-start | bytes 24580
  20.8 11.4 %copy-start.16 = (bf16[64,64]{1,0:T(8,128)(2,1)S(1)}, bf16[64,64]{1,0:T(8,128)(2,1)}, u32[]{:S(2)}) copy-start(bf16[64,64]{1,0:T(8,128)(2,1)} %param.16) | copy-start | bytes 24580
  20.8 11.4 %copy-start.30 = (f32[64]{0:T(128)S(1)}, f32[64]{0:T(128)}, u32[]{:S(2)}) copy-start(f32[64]{0:T(128)} %param.15) | copy-start | bytes 772
  20.8 11.4 %copy-start.31 = (s32[292]{0:T(512)S(1)}, s32[292]{0:T(512)}, u32[]{:S(2)}) copy-start(s32[292]{0:T(512)} %param.13) | copy-start | bytes 3508
  21.0 8.4 %collective-permute-start.3 = (bf16[1,64,73,2,1,4]{2,1,5,0,3,4:T(8,128)(2,1)S(1)}, bf16[1,64,73,2,1,4]{2,1,5,0,3,4:T(8,128)(2,1)S(1)}, u32[]{:S(2)}, u32[]{:S(2)}) collective-permute-start(bf16[1,64,73,2,1,4]{2,1,5,0,3,4:T(8,128)(2,1)S(1)} %get-tuple-element.167), channel_id=1, source_target_pairs={{0,8},{4,12},{8,0},{12,4},{1,9},{5,13},{9,1},{13,5},{2,10},{6,14},... | collective-permute-start | bytes 224264 | tf_op jit(solution)/shard_map/ppermute | solution.py:26
  23.7 7.7 %collective-permute-start.4 = (bf16[1,64,73,2,1,4]{2,1,5,0,3,4:T(8,128)(2,1)S(1)}, bf16[1,64,73,2,1,4]{2,1,5,0,3,4:T(8,128)(2,1)S(1)}, u32[]{:S(2)}, u32[]{:S(2)}) collective-permute-start(bf16[1,64,73,2,1,4]{2,1,5,0,3,4:T(8,128)(2,1)S(1)} %get-tuple-element.166), channel_id=1, source_target_pairs={{0,12},{4,0},{8,4},{12,8},{1,13},{5,1},{9,5},{13,9},{2,14},{6,2},{... | collective-permute-start | bytes 224264 | tf_op jit(solution)/shard_map/ppermute | solution.py:26
  51.3 4.3 %copy-start.19 = (bf16[2,4,292,64]{2,3,1,0:T(8,128)(2,1)}, bf16[2,4,292,64]{2,3,1,0:T(8,128)(2,1)S(1)}, u32[]{:S(2)}) copy-start(bf16[2,4,292,64]{2,3,1,0:T(8,128)(2,1)S(1)} %fusion.295) | copy-start | bytes 897028 | tf_op jit(solution)/shard_map/while
  75.4 4.3 %copy-start.19 = (bf16[2,4,292,64]{2,3,1,0:T(8,128)(2,1)}, bf16[2,4,292,64]{2,3,1,0:T(8,128)(2,1)S(1)}, u32[]{:S(2)}) copy-start(bf16[2,4,292,64]{2,3,1,0:T(8,128)(2,1)S(1)} %fusion.295) | copy-start | bytes 897028 | tf_op jit(solution)/shard_map/while
  80.3 7.9 %copy-start.26 = (f32[2,64,64]{2,1,0:T(8,128)S(1)}, f32[2,64,64]{2,1,0:T(8,128)}, u32[]{:S(2)}) copy-start(f32[2,64,64]{2,1,0:T(8,128)} %get-tuple-element.99) | copy-start | bytes 98308
  80.3 8.5 %copy-start.29 = (f32[2,64,64]{2,1,0:T(8,128)S(1)}, f32[2,64,64]{2,1,0:T(8,128)}, u32[]{:S(2)}) copy-start(f32[2,64,64]{2,1,0:T(8,128)} %get-tuple-element.100) | copy-start | bytes 98308
  80.3 10.6 %copy-start.23 = (f32[2,64,64]{2,1,0:T(8,128)S(1)}, f32[2,64,64]{2,1,0:T(8,128)}, u32[]{:S(2)}) copy-start(f32[2,64,64]{2,1,0:T(8,128)} %get-tuple-element.102) | copy-start | bytes 98308
  83.2 14.3 %all-to-all-start = ((bf16[4,2,18688]{2,1,0:T(2,128)(2,1)}), bf16[4,2,18688]{2,1,0:T(2,128)(2,1)S(1)}, u32[]{:S(2)}, u32[]{:S(2)}) async-start(bf16[4,2,18688]{2,1,0:T(2,128)(2,1)} %reshape.100), calls=%async_computation | async-start | bytes 598016 | tf_op jit(solution)/shard_map/all_to_all | solution.py:161
  88.2 96.8 %all-reduce.8.cloned.1.call-start = ((), (), s32[]{:S(2)}) async-start(), calls=%async_computation.2 | async-start | bytes 263168 | tf_op jit(solution)/shard_map/psum | solution.py:174
  92.1 189.9 %all-reduce.6.cloned.1.call-start = ((), (), s32[]{:S(2)}) async-start(), calls=%async_computation.1 | async-start | bytes 589824 | tf_op jit(solution)/shard_map/psum | solution.py:174
  102.4 5.5 %copy-start.20 = (f32[64,64,9]{1,0,2:T(8,128)}, f32[64,64,9]{1,0,2:T(8,128)S(1)}, u32[]{:S(2)}) copy-start(f32[64,64,9]{1,0,2:T(8,128)S(1)} %fusion.104) | copy-start | bytes 442372
  102.4 5.9 %collective-permute-start.6 = (bf16[64,73,1,16]{1,0,3,2:T(8,128)(2,1)S(1)}, bf16[64,73,1,16]{1,0,3,2:T(8,128)(2,1)S(1)}, u32[]{:S(2)}, u32[]{:S(2)}) collective-permute-start(bf16[64,73,1,16]{1,0,3,2:T(8,128)(2,1)S(1)} %get-tuple-element.165), channel_id=1, source_target_pairs={{1,0},{2,1},{3,2},{5,4},{6,5},{7,6},{9,8},{10,9},{11,10},{13,12},{... | collective-permute-start | bytes 448520 | tf_op jit(solution)/shard_map/ppermute | solution.py:41
  103.7 5.3 %collective-permute-start.5 = (bf16[64,73,1,16]{1,0,3,2:T(8,128)(2,1)S(1)}, bf16[64,73,1,16]{1,0,3,2:T(8,128)(2,1)S(1)}, u32[]{:S(2)}, u32[]{:S(2)}) collective-permute-start(bf16[64,73,1,16]{1,0,3,2:T(8,128)(2,1)S(1)} %get-tuple-element.164), channel_id=1, source_target_pairs={{0,1},{1,2},{2,3},{4,5},{5,6},{6,7},{8,9},{9,10},{10,11},{12,13},{... | collective-permute-start | bytes 448520 | tf_op jit(solution)/shard_map/ppermute | solution.py:39
  (36 other events, 61.8 us)
Sparse Core Ops, SparseCore 0:
  93.7 91.2 all-reduce.7
  188.9 93.0 all-reduce.5
